TPU v7x, 32 devices: a whole 2x2x4 slice. The times are simulated.
32 devices in a mesh: seg: 8 (over z, x), rep: 4 (over y, core).
Axes of the slice: x: 2, y: 2, z: 4, core: 2. Of those that a mesh axis runs over, the one named last changes fastest.
Arguments:
- decoder_rows: bfloat16 [256, 4096], P('rep', 'seg'), may hold values from -2000 to 2000
- norm_gain: float32 [4096], replicated, may hold values from 0.5 to 1.5
- query_weight: bfloat16 [4096, 4096], P('rep', 'seg'), may hold values from -1 to 1
- key_codes: bfloat16 [4, 4096, 4096], P('rep', 'seg'), may hold values from -127 to 127, as said below
- key_scale: float32 [4, 32, 64], P('rep', 'seg'), may hold values from 0.5 to 1.5
- value_codes: bfloat16 [4, 4096, 4096], P('rep', 'seg'), may hold values from -6 to 6
- value_scale: float32 [4, 32, 64], P('rep', 'seg'), may hold values from 0.5 to 2
- enc_lengths: int32 [4], P('rep'), may hold values from 1024 to 4096
- output_weight: bfloat16 [4096, 4096], P('seg', 'rep'), may hold values from -0.09375 to 0.09375
Outputs:
- update: bfloat16 [256, 4096], P('rep', 'seg')
Inputs may be any that keep to these rules, and one draw needn't show every extreme that they name: `key_codes`: codes of a block times its scale give the cached keys.
All inputs are finite; a program needn't handle non-finite values.
Results may differ from a plain program's by a relative error of at most 0.011.
Values may be sent and summed in bfloat16 or wider, within the bound.
A program may use at most 64 MiB of HBM per device.

v0:
```python
import jax
import jax.numpy as jnp
from jax import lax
from jax.sharding import PartitionSpec as P


def per_device(
    decoder_rows,
    norm_gain,
    query_weight,
    key_codes,
    key_scale,
    value_codes,
    value_scale,
    enc_lengths,
    output_weight,
):
    gathered = lax.all_gather(decoder_rows, "seg", axis=1, tiled=True)
    widened = gathered.astype(jnp.float32)
    variance = jnp.mean(widened * widened, axis=-1, keepdims=True)
    normed = (widened * lax.rsqrt(variance + 1e-06) * norm_gain[None, :]).astype(jnp.bfloat16)
    query_own = jnp.dot(
        normed,
        lax.all_gather(query_weight, "rep", axis=0, tiled=True),
        preferred_element_type=jnp.float32,
    ).astype(jnp.bfloat16)
    queries = lax.all_gather(query_own, "seg", axis=1, tiled=True)
    docs_here, seg_length, inner_width = key_codes.shape
    head_count = key_scale.shape[2]
    head_dim = inner_width // head_count
    block_length = seg_length // key_scale.shape[1]
    per_doc = queries.shape[0] // docs_here
    row_count = docs_here * per_doc
    first_pos = lax.axis_index("seg") * seg_length
    positions = first_pos + jnp.arange(seg_length, dtype=jnp.int32)

    def one_doc(group_members):
        (
            document_query,
            document_keys,
            document_values,
            document_key_scale,
            document_value_scale,
            document_length,
        ) = group_members
        split_query = document_query.reshape(per_doc, head_count, head_dim)
        split_keys = document_keys.reshape(seg_length, head_count, head_dim)
        split_values = document_values.reshape(seg_length, head_count, head_dim)
        attention_scores = jnp.einsum(
            "qhd,khd->qhk", split_query, split_keys, preferred_element_type=jnp.float32
        )
        key_multiplier = jnp.repeat(document_key_scale, block_length, axis=0).T
        value_factor = jnp.repeat(document_value_scale, block_length, axis=0).T
        attention_scores = attention_scores * key_multiplier[None]
        usable = (positions < document_length)[None, None, :]
        attention_scores = jnp.where(usable, attention_scores, jnp.float32(-1e30))
        peaks = jnp.max(attention_scores, axis=-1)
        weights = jnp.where(usable, jnp.exp(attention_scores - peaks[..., None]), jnp.float32(0.0))
        totals = jnp.sum(weights, axis=-1)
        scaled = (weights * value_factor[None]).astype(jnp.bfloat16)
        attended = jnp.einsum(
            "qhk,khd->qhd", scaled, split_values, preferred_element_type=jnp.float32
        )
        return (peaks, totals, attended.reshape(per_doc, inner_width))

    query_docs = queries.reshape(docs_here, per_doc, inner_width)
    peaks, totals, outputs = lax.map(
        one_doc, (query_docs, key_codes, value_codes, key_scale, value_scale, enc_lengths)
    )
    peaks = peaks.reshape(row_count, head_count)
    totals = totals.reshape(row_count, head_count)
    outputs = outputs.reshape(row_count, inner_width)
    seg_count = lax.axis_size("seg")
    own_heads = head_count // seg_count
    received = (
        lax.all_to_all(peaks[None], "seg", split_axis=2, concat_axis=0, tiled=True),
        lax.all_to_all(totals[None], "seg", split_axis=2, concat_axis=0, tiled=True),
        lax.all_to_all(outputs[None], "seg", split_axis=2, concat_axis=0, tiled=True),
    )
    peak_all, total_all, out_all = received
    largest = jnp.max(peak_all, axis=0)
    factor = jnp.exp(peak_all - largest[None])
    denominator = jnp.sum(factor * total_all, axis=0)
    numerator = jnp.sum(
        out_all.reshape(seg_count, row_count, own_heads, head_dim) * factor[..., None], axis=0
    )
    attn_own = (
        (numerator / denominator[..., None])
        .reshape(row_count, own_heads * head_dim)
        .astype(jnp.bfloat16)
    )
    partial_terms = jnp.dot(
        attn_own,
        lax.all_gather(output_weight, "rep", axis=1, tiled=True),
        preferred_element_type=jnp.float32,
    )
    return lax.psum_scatter(partial_terms, "seg", scatter_dimension=1, tiled=True).astype(
        jnp.bfloat16
    )


def solution(mesh):
    placed = (
        P("rep", "seg"),
        P(),
        P("rep", "seg"),
        P("rep", "seg", None),
        P("rep", "seg", None),
        P("rep", "seg", None),
        P("rep", "seg", None),
        P("rep"),
        P("seg", "rep"),
    )
    return jax.shard_map(
        per_device, mesh=mesh, in_specs=placed, out_specs=P("rep", "seg"), check_vma=False
    )
```

profile of v0, /device:TPU:5, one launch (start us, length us, event | category | flops | bytes accessed | tf_op | source)
XLA Modules:
  0.0 247.4 jit_solution(3098906229739473497)
XLA Ops:
  6.5 0.0 all-gather.3.cloned.1.call-start
  6.5 0.7 all-gather.3.cloned.1.call-update
  7.3 0.0 all-gather.5.cloned.1.call-start
  7.3 0.7 all-gather.5.cloned.1.call-update
  8.0 0.8 copy.36
  8.8 0.1 broadcast_in_dim.60
  9.6 0.0 copy-start.1
  9.6 0.0 copy-start.2
  9.6 6.6 %copy.34 = bf16[1,512,4096]{1,2,0:T(8,128)(2,1)} copy(bf16[1,512,4096]{2,1,0:T(8,128)(2,1)} %param.12) | data formatting | bytes 8388608 | tf_op args[3]
  16.2 0.0 copy-done.1
  16.2 26.1 %all_gather.12 = bf16[64,4096]{1,0:T(8,128)(2,1)S(1)} all-gather(bf16[64,512]{1,0:T(8,128)(2,1)S(1)} %copy-done.1), channel_id=1, replica_groups=mesh['seg'=8,'rep'=4] {'seg'}, dimensions={1}, use_global_device_ids=true | all-gather | bytes 589824 | tf_op jit(solution)/shard_map/all_gather | solution.py:18
  42.3 0.2 fusion.13
  42.5 1.3 all-gather.3.cloned.1.call-done
  43.9 0.0 copy-done.2
  43.9 3.1 %convolution_convert_fusion = bf16[64,512]{1,0:T(8,128)(2,1)S(1)} fusion(bf16[4096,512]{1,0:T(8,128)(2,1)} %all-gather.3.cloned.1.call-done, bf16[64,4096]{1,0:T(8,128)(2,1)S(1)} %all_gather.12, f32[4096]{0:T(1024)S(1)} %copy-done.2, f32[64]{0:T(128)S(1)} %add_rsqrt_fusion), kind=kOutput, calls=%fused_computation.20 | convolution fusion | flops 269516800 | bytes 4800768 | tf_op jit(solution)/shard_map/dot_general | solution.py:22
  46.9 26.0 %all_gather.14 = bf16[64,4096]{1,0:T(8,128)(2,1)S(1)} all-gather(bf16[64,512]{1,0:T(8,128)(2,1)S(1)} %convolution_convert_fusion), channel_id=1, replica_groups=mesh['seg'=8,'rep'=4] {'seg'}, dimensions={1}, use_global_device_ids=true | all-gather | bytes 589824 | tf_op jit(solution)/shard_map/all_gather | solution.py:27
  72.9 1.1 reshape.64
  74.1 4.2 %bitcast_reduce_fusion = (f32[64,64]{0,1:T(8,128)S(1)}, f32[64,64,512]{2,1,0:T(8,128)S(1)}) fusion(f32[64,512]{1,0:T(8,128)S(1)} %bitcast.79, pred[512]{0:T(512)(128)(4,1)S(1)} %add_compare_fusion, bf16[512,64,64]{0,2,1:T(8,128)(2,1)} %bitcast.75, bf16[64,64,64]{2,1,0:T(8,128)(2,1)S(1)} %reshape.64), kind=kOutput, calls=%fused_computation.1 | convolution fusion | flops 274722816 | bytes 13255168 | tf_op jit(solution)/shard_map/while/body/eval_jaxpr/qhd,khd->qhk/dot_general | solution.py:49
  78.2 0.0 copy-start
  78.2 2.8 %fusion.2 = f32[64,64]{0,1:T(8,128)S(1)} fusion(f32[64,64,512]{2,1,0:T(8,128)S(1)} %get-tuple-element.28, f32[64,64]{0,1:T(8,128)S(1)} %get-tuple-element.27, f32[64,512]{1,0:T(8,128)S(1)} %bitcast.80, pred[512]{0:T(512)(128)(4,1)S(1)} %add_compare_fusion), kind=kLoop, calls=%fused_computation.6 | loop fusion | flops 10481664 | bytes 8552960 | tf_op jit(solution)/shard_map/while/body/eval_jaxpr/reduce_sum | solution.py:59
  81.1 0.4 copy-done
  81.5 0.5 broadcast.37
  82.0 0.7 reduce.4
  82.7 0.7 reshape.73
  83.4 5.2 %all-to-all-start.2 = ((f32[8,1,512]{2,1,0:T(1,128)}), f32[8,1,512]{2,1,0:T(1,128)S(1)}, u32[]{:S(2)}, u32[]{:S(2)}) async-start(f32[8,1,512]{2,1,0:T(1,128)} %reshape.73), calls=%async_computation.2 | async-start | bytes 32768 | tf_op jit(solution)/shard_map/all_to_all | solution.py:77
  88.6 0.0 copy-start.3
  88.6 6.5 %copy.39 = bf16[1,512,4096]{1,2,0:T(8,128)(2,1)} copy(bf16[1,512,4096]{2,1,0:T(8,128)(2,1)} %param.14) | data formatting | bytes 8388608 | tf_op args[5]
  95.1 0.0 copy-done.3
  95.1 0.1 copy.38
  95.2 0.1 broadcast_in_dim.63
  95.3 0.7 reduce.6
  96.0 0.7 reshape.71
  96.7 0.0 all-to-all-done.2
  96.7 5.4 %all-to-all-start.1 = ((f32[8,1,512]{2,1,0:T(1,128)}), f32[8,1,512]{2,1,0:T(1,128)S(1)}, u32[]{:S(2)}, u32[]{:S(2)}) async-start(f32[8,1,512]{2,1,0:T(1,128)} %reshape.71), calls=%async_computation.1 | async-start | bytes 32768 | tf_op jit(solution)/shard_map/all_to_all | solution.py:76
  102.1 8.5 %fusion.12 = f32[64,64,64]{2,0,1:T(8,128)} fusion(bf16[512,64,64]{0,2,1:T(8,128)(2,1)} %bitcast.78, f32[64,64,512]{2,1,0:T(8,128)} %copy-done, f32[64,512]{1,0:T(8,128)S(1)} %bitcast.88, f32[64,64]{0,1:T(8,128)S(1)} %get-tuple-element.27, f32[64,512]{1,0:T(8,128)S(1)} %bitcast.81, pred[512]{0:T(512)(128)(4,1)S(1)} %add_compare_fusion), kind=kOutput, calls=%fused_computation.17 | convolution fusion | flops 281018368 | bytes 13910528 | tf_op jit(solution)/shard_map/while/body/eval_jaxpr/qhk,khd->qhd/dot_general | solution.py:61
  110.6 1.9 copy.42
  112.6 19.3 %reduce.2 = f32[4096,64]{1,0:T(8,128)} reduce(f32[4096,1,64]{2,1,0:T(1,128)S(1)} %bitcast.77, f32[]{:T(128)} %broadcast.37), dimensions={1}, to_apply=%bitcast.59.reduce_sub_computation | reduce | bytes 2097156
  131.9 3.4 %reshape.69 = f32[8,1,32768]{2,1,0:T(1,128)} reshape(f32[4096,64]{1,0:T(8,128)} %reduce.2) | data formatting | bytes 2097152
  135.3 0.0 all-to-all-done.1
  135.3 5.4 %all-to-all-start = ((f32[8,1,32768]{2,1,0:T(1,128)}), f32[8,1,32768]{2,1,0:T(1,128)S(1)}, u32[]{:S(2)}, u32[]{:S(2)}) async-start(f32[8,1,32768]{2,1,0:T(1,128)} %reshape.69), calls=%async_computation | async-start | bytes 2097152 | tf_op jit(solution)/shard_map/all_to_all | solution.py:78
  140.7 0.3 reduce-scatter.2.cloned.1.call-start
  141.0 0.7 reduce.5
  141.6 0.1 reshape.74
  141.7 0.7 reduce.7
  142.4 0.1 reshape.72
  142.5 13.2 %all-to-all-done = f32[8,1,32768]{2,1,0:T(1,128)S(1)} async-done(((f32[8,1,32768]{2,1,0:T(1,128)}), f32[8,1,32768]{2,1,0:T(1,128)S(1)}, u32[]{:S(2)}, u32[]{:S(2)}) %all-to-all-start) | async-done | bytes 1048608 | tf_op jit(solution)/shard_map/all_to_all | solution.py:78
  155.7 3.1 %reduce.3 = f32[8,32768]{1,0:T(8,128)S(1)} reduce(f32[8,1,32768]{2,1,0:T(1,128)S(1)} %all-to-all-done, f32[]{:T(128)} %broadcast.37), dimensions={1}, to_apply=%all_to_all.37.reduce_sub_computation | reduce | bytes 2097156 | tf_op jit(solution)/shard_map/all_to_all | solution.py:78
  158.9 2.6 %reshape.70 = f32[4096,1,64]{2,1,0:T(1,128)S(1)} reshape(f32[8,32768]{1,0:T(8,128)S(1)} %reduce.3) | data formatting | bytes 2097152
  161.5 0.2 fusion.11
  161.7 0.0 all-gather.5.cloned.1.call-done
  161.8 4.0 %fusion.24 = f32[64,4096]{1,0:T(8,128)} fusion(bf16[64,512]{0,1:T(8,128)(2,1)S(1)} %fusion.21, bf16[512,4096]{1,0:T(8,128)(2,1)} %all-gather.5.cloned.1.call-done), kind=kOutput, calls=%fused_computation.38 | convolution fusion | flops 268435456 | bytes 5308416 | tf_op jit(solution)/shard_map/dot_general | solution.py:92
  165.8 0.0 reduce-scatter.2.cloned.1.call-update
  165.8 73.5 %reduce-scatter.2.cloned.1.call-done = f32[64,512]{1,0:T(8,128)} async-done(((f32[64,4096]{1,0:T(8,128)}), f32[64,512]{1,0:T(8,128)}) %reduce-scatter.2.cloned.1.call-update) | async-done | bytes 131088 | tf_op jit(solution)/shard_map/reduce_scatter | solution.py:97
  239.3 1.5 convert_element_type.24
  (7 shorter events, 0.1 us)
Async XLA Ops:
  6.5 37.3 %all-gather.3.cloned.1.call-start = ((), (), s32[]{:S(2)}) async-start(), calls=%async_computation.4 | async-start | bytes 5242880 | tf_op jit(solution)/shard_map/all_gather | solution.py:24
  7.3 154.5 %all-gather.5.cloned.1.call-start = ((), (), s32[]{:S(2)}) async-start(), calls=%async_computation.5 | async-start | bytes 5242880 | tf_op jit(solution)/shard_map/all_gather | solution.py:94
  9.6 6.6 %copy-start.1 = (bf16[64,512]{1,0:T(8,128)(2,1)S(1)}, bf16[64,512]{1,0:T(8,128)(2,1)}, u32[]{:S(2)}) copy-start(bf16[64,512]{1,0:T(8,128)(2,1)} %param.9) | copy-start | bytes 196612
  9.6 34.3 %copy-start.2 = (f32[4096]{0:T(1024)S(1)}, f32[4096]{0:T(1024)}, u32[]{:S(2)}) copy-start(f32[4096]{0:T(1024)} %param.10) | copy-start | bytes 49156
  78.2 3.2 %copy-start = (f32[64,64,512]{2,1,0:T(8,128)}, f32[64,64,512]{2,1,0:T(8,128)S(1)}, u32[]{:S(2)}) copy-start(f32[64,64,512]{2,1,0:T(8,128)S(1)} %get-tuple-element.28) | copy-start | bytes 25165828
  83.4 13.3 %all-to-all-start.2 = ((f32[8,1,512]{2,1,0:T(1,128)}), f32[8,1,512]{2,1,0:T(1,128)S(1)}, u32[]{:S(2)}, u32[]{:S(2)}) async-start(f32[8,1,512]{2,1,0:T(1,128)} %reshape.73), calls=%async_computation.2 | async-start | bytes 32768 | tf_op jit(solution)/shard_map/all_to_all | solution.py:77
  88.6 6.5 %copy-start.3 = (f32[1,4,64]{2,1,0:T(4,128)S(1)}, f32[1,4,64]{2,1,0:T(4,128)}, u32[]{:S(2)}) copy-start(f32[1,4,64]{2,1,0:T(4,128)} %param.15) | copy-start | bytes 3076
  96.7 38.6 %all-to-all-start.1 = ((f32[8,1,512]{2,1,0:T(1,128)}), f32[8,1,512]{2,1,0:T(1,128)S(1)}, u32[]{:S(2)}, u32[]{:S(2)}) async-start(f32[8,1,512]{2,1,0:T(1,128)} %reshape.71), calls=%async_computation.1 | async-start | bytes 32768 | tf_op jit(solution)/shard_map/all_to_all | solution.py:76
  135.3 20.5 %all-to-all-start = ((f32[8,1,32768]{2,1,0:T(1,128)}), f32[8,1,32768]{2,1,0:T(1,128)S(1)}, u32[]{:S(2)}, u32[]{:S(2)}) async-start(f32[8,1,32768]{2,1,0:T(1,128)} %reshape.69), calls=%async_computation | async-start | bytes 2097152 | tf_op jit(solution)/shard_map/all_to_all | solution.py:78
  140.7 98.6 %reduce-scatter.2.cloned.1.call-start = ((), (), s32[]{:S(2)}) async-start(), calls=%async_computation.6 | async-start | bytes 1179648 | tf_op jit(solution)/shard_map/reduce_scatter | solution.py:97
Sparse Core Ops, SparseCore 0:
  8.9 34.9 all-gather.2
  45.4 34.4 all-gather.4
  166.0 73.3 reduce-scatter.1
where the time goes:
time: 252 us; the launch traced here: 247 us
  waiting for transfers between devices  89.5 us (36%)
  blocking collectives  52.1 us (21%)
  other arithmetic  30 us (12%)
  local copies, waits for them, and re-layouts  25.7 us (10%)
  matrix products  19.8 us (8%)
  starting transfers between devices  16.4 us (7%)
  between operations  14 us (6%)
    reduce_scatter x1, waiting for transfers between devices, per_device(): lax.psum_scatter(partial_terms, 'seg', scatter_dimension=1, tiled=True)  73.5 us
    all_gather x1, blocking collectives, per_device(): gathered = lax.all_gather(decoder_rows, 'seg', axis=1, tiled=True)  26.1 us
    all_gather x1, blocking collectives, per_device(): queries = lax.all_gather(query_own, 'seg', axis=1, tiled=True)  26 us
    unnamed x19, local copies, waits for them, and re-layouts  21.5 us
    unnamed x3, other arithmetic  20.7 us
    all_to_all x1, waiting for transfers between devices, per_device(): lax.all_to_all(outputs[None], 'seg', split_axis=2, concat_axis=0, tiled=T...  13.2 us
    dot_general x1, matrix products, one_doc(): jnp.einsum('qhk,khd->qhd', scaled, split_values, preferred_element_type=j...  8.51 us
    all_to_all x1, starting transfers between devices, per_device(): lax.all_to_all(outputs[None], 'seg', split_axis=2, concat_axis=0, tiled=T...  5.44 us
  transfers between devices with their start and end apart: 6, of which 3 were waited for; matrix products, arithmetic and copies ran while one was open for 28% of the time, Pallas kernels for 0%

commit v1 on v0

v1 whole, which is shorter than its diff:
```python
import functools

import jax
import jax.numpy as jnp
from jax import lax
from jax.experimental import pallas as pl
from jax.experimental.pallas import tpu as pltpu
from jax.sharding import PartitionSpec as P

F32 = jnp.float32
BF16 = jnp.bfloat16
LANES = 128
PART = 16
INNER_RING = 2


def spread(value):
    high = value.astype(BF16).astype(F32)
    rest = value - high
    mid = rest.astype(BF16).astype(F32)
    low = (rest - mid).astype(BF16).astype(F32)
    packed = high + pltpu.roll(mid, PART, 1) + pltpu.roll(low, 2 * PART, 1)
    return packed.astype(BF16)


def gather_spread(packed):
    wide = packed.astype(F32)
    low = pltpu.roll(wide, LANES - 2 * PART, 1)
    mid = pltpu.roll(wide, LANES - PART, 1)
    return wide + (mid + low)


def kernel(
    nseg,
    nrep,
    heads,
    rows_ref,
    gain_ref,
    wq_hbm,
    k_hbm,
    ks_ref,
    v_hbm,
    vs_ref,
    len_ref,
    wo_hbm,
    out_ref,
    wq,
    wo,
    kbuf,
    vbuf,
    xg,
    y,
    pq,
    pq_in,
    qs,
    oout,
    oin,
    ag,
    pf,
    pf32,
    rbuf,
    sbuf,
    fbuf,
    fin,
    land,
    local_sem,
    send_sem,
    recv_sem,
):
    seg = lax.axis_index("seg")
    rep = lax.axis_index("rep")
    nrow, c = rows_ref.shape
    width = gain_ref.shape[1]
    m = nseg // nrep
    nb = INNER_RING
    na = nseg // nb
    a, b = seg // nb, seg % nb
    hd = wq.shape[1] * nseg // heads
    hpl = LANES // hd
    hpb = c // hd
    pairs = c // LANES
    tokens = kbuf.shape[0]
    blocks = ks_ref.shape[1]
    blen = tokens // blocks

    state = {"k": 0}
    started = []

    def send(src, dst, to_rep, to_seg, start=True):
        k = state["k"]
        state["k"] += 1
        copy = pltpu.make_async_remote_copy(
            src_ref=src,
            dst_ref=dst,
            send_sem=send_sem.at[k],
            recv_sem=recv_sem.at[k],
            device_id={"rep": to_rep, "seg": to_seg},
            device_id_type=pl.DeviceIdType.MESH,
        )
        if start:
            copy.start()
            started.append(copy)
        return copy

    loads = {}
    lk = 0

    def load(name, src, dst):
        nonlocal lk
        copy = pltpu.make_async_copy(src, dst, local_sem.at[lk])
        lk += 1
        copy.start()
        loads[name] = copy

    load("wq", wq_hbm, wq)
    load("k", k_hbm.at[0], kbuf)
    load("v", v_hbm.at[0], vbuf)
    load("wo", wo_hbm, wo)

    to_rep, to_seg = seg // m, rep * m + seg % m
    alone = to_rep == rep
    barrier = pltpu.get_barrier_semaphore()

    def greet(r, s):
        pl.semaphore_signal(
            barrier, inc=1, device_id={"rep": r, "seg": s}, device_id_type=pl.DeviceIdType.MESH
        )

    for d in range(1, nseg):
        greet(rep, lax.rem(seg + d, nseg))
    for d in range(1, nrep):
        greet(lax.rem(rep + d, nrep), seg)

    @pl.when(jnp.logical_not(alone))
    def _():
        greet(to_rep, to_seg)

    pl.semaphore_wait(barrier, jnp.where(alone, nseg + nrep - 2, nseg + nrep - 1))

    first = send(rows_ref, xg.at[to_seg], to_rep, to_seg, start=False)

    @pl.when(jnp.logical_not(alone))
    def _():
        first.start()
        first.wait()

    @pl.when(alone)
    def _():
        xg[seg] = rows_ref[...]

    def slot(ai, bi):
        return ai * nb + bi

    def near(d):
        return lax.rem(a + d, na)

    def from_(d):
        return lax.rem(a + na - d, na)

    def gather_start(buf):
        across = [
            send(buf.at[seg], buf.at[seg], rep, slot(a, lax.rem(b + e, nb))) for e in range(1, nb)
        ]
        along = [send(buf.at[seg], buf.at[seg], rep, slot(near(d), b)) for d in range(1, na)]
        return across, along

    def pass_on(buf, d):
        block = slot(from_(d), b)
        return [
            send(buf.at[block], buf.at[block], rep, slot(a, lax.rem(b + e, nb)))
            for e in range(1, nb)
        ]

    def gather(buf, use):
        across, along = gather_start(buf)
        use(seg)
        waiting = [(copy, slot(a, lax.rem(b + nb - e, nb))) for e, copy in enumerate(across, 1)]
        for d, copy in enumerate(along, 1):
            copy.wait_recv()
            passed = pass_on(buf, d)
            for other, block in waiting:
                other.wait_recv()
                use(block)
            use(slot(from_(d), b))
            waiting = [
                (other, slot(from_(d), lax.rem(b + nb - e, nb))) for e, other in enumerate(passed, 1)
            ]
        for other, block in waiting:
            other.wait_recv()
            use(block)

    gather(xg, lambda block: None)

    lane = lax.broadcasted_iota(jnp.int32, (nrow, LANES), 1)
    for doc in range(nrep):
        total = jnp.zeros((nrow, 1), F32)
        for j in range(m):
            wide = xg[doc * m + j].astype(F32)
            total = total + jnp.sum(wide * wide, axis=1, keepdims=True)
            at = pl.multiple_of((rep * m + j) * c, LANES)
            y[doc * nrow : (doc + 1) * nrow, j * c : (j + 1) * c] = (
                wide * gain_ref[0:1, pl.ds(at, c)]
            ).astype(BF16)
        pq[doc, :, c:] = spread(jnp.where(lane == 0, total, 0.0))
    loads["wq"].wait()
    part = jnp.dot(y[...], wq[...], preferred_element_type=F32)
    for doc in range(nrep):
        pq[doc, :, :c] = part[doc * nrow : (doc + 1) * nrow].astype(BF16)
    sums = []
    for d in range(1, nrep):
        other = lax.rem(rep + d, nrep)
        sums.append(send(pq.at[other], pq_in.at[d - 1], other, seg))
    acc = pq[rep, :, :c].astype(F32)
    squares = gather_spread(pq[rep, :, c:])
    for d, copy in enumerate(sums):
        copy.wait_recv()
        acc = acc + pq_in[d, :, :c].astype(F32)
        squares = squares + gather_spread(pq_in[d, :, c:])
    inverse = lax.rsqrt(squares[:, 0:1] / width + 1e-06)
    qs[seg] = (acc * inverse).astype(BF16)

    loads["k"].wait()
    loads["v"].wait()
    position = seg * tokens + lax.broadcasted_iota(jnp.int32, (1, tokens), 1)
    bias = jnp.where(position < len_ref[0], 0.0, -1e30).astype(F32)
    turns = []

    def attend(block):
        own_turn = not turns

        def one(t, stats):
            at = pl.multiple_of(t * LANES, LANES)
            wat = pl.multiple_of(block * c + t * LANES, LANES)
            q = qs[block, :, pl.ds(at, LANES)]
            stacked = jnp.concatenate(
                [
                    jnp.where((lane >= i * hd) & (lane < (i + 1) * hd), q, jnp.zeros_like(q))
                    for i in range(hpl)
                ],
                axis=0,
            )
            scores = lax.dot_general(
                stacked,
                kbuf[:, pl.ds(wat, LANES)],
                (((1,), (1,)), ((), ())),
                preferred_element_type=F32,
            )
            scaled_rows = []
            for i in range(hpl):
                head = block * hpb + t * hpl + i
                pieces = []
                for n in range(blocks):
                    cut = slice(n * blen, (n + 1) * blen)
                    pieces.append(
                        scores[i * nrow : (i + 1) * nrow, cut] * ks_ref[0, n, head]
                        + bias[:, cut]
                    )
                top = functools.reduce(jnp.maximum, pieces)
                peak = jnp.max(top, axis=1, keepdims=True)
                weights = [jnp.exp(piece - peak) for piece in pieces]
                whole = jnp.sum(functools.reduce(jnp.add, weights), axis=1, keepdims=True)
                scaled_rows.append(
                    jnp.concatenate(
                        [(w * vs_ref[0, n, head]).astype(BF16) for n, w in enumerate(weights)],
                        axis=1,
                    )
                )
                index = t * hpl + i
                stats = jnp.where(lane == index, peak, stats)
                stats = jnp.where(lane == LANES // 2 + index, whole, stats)
            summed = jnp.dot(
                jnp.concatenate(scaled_rows, axis=0),
                vbuf[:, pl.ds(wat, LANES)],
                preferred_element_type=F32,
            )
            mine = summed[:nrow]
            for i in range(1, hpl):
                mine = jnp.where(lane >= i * hd, summed[i * nrow : (i + 1) * nrow], mine)
            oout[block, :, pl.ds(at, LANES)] = mine.astype(BF16)
            return stats

        stats = lax.fori_loop(
            0, pairs, one, jnp.zeros((nrow, LANES), F32), unroll=2 if pairs % 2 == 0 else 1
        )
        oout[block, :, c:] = spread(stats)
        if own_turn:
            turns.append(None)
        else:
            turns.append(send(oout.at[block], oin.at[len(turns) - 1], rep, block))

    gather(qs, attend)

    for copy in turns[1:]:
        copy.wait_recv()
    parts = [oout.at[seg]] + [oin.at[i] for i in range(nseg - 1)]
    stats = [gather_spread(part_ref[:, c:]) for part_ref in parts]
    largest = functools.reduce(jnp.maximum, stats)
    factors = [jnp.exp(s - largest) for s in stats]
    denominator = functools.reduce(
        jnp.add, [f * pltpu.roll(s, LANES // 2, 1) for f, s in zip(factors, stats)]
    )
    factors = [f / denominator for f in factors]
    for t in range(pairs):
        cut = slice(t * LANES, (t + 1) * LANES)
        total = None
        for f, part_ref in zip(factors, parts):
            g = f[:, t * hpl : t * hpl + 1]
            for i in range(1, hpl):
                g = jnp.where(lane >= i * hd, f[:, t * hpl + i : t * hpl + i + 1], g)
            term = g * part_ref[:, cut].astype(F32)
            total = term if total is None else total + term
        ag[rep, :, cut] = total.astype(BF16)
    shared = [
        send(ag.at[rep], ag.at[rep], lax.rem(rep + d, nrep), seg) for d in range(1, nrep)
    ]
    loads["wo"].wait()
    for copy in shared:
        copy.wait_recv()

    part = jnp.dot(
        ag[...].reshape(nrep * nrow, c), wo[...], preferred_element_type=F32
    )
    for p in range(nseg):
        doc, j = p // m, p % m
        piece = part[doc * nrow : (doc + 1) * nrow, j * c : (j + 1) * c]
        pf32[p] = piece
        pf[p] = piece.astype(BF16)
    order = list(range(1, na)) + [0]
    crossed = {}
    for d in order:
        crossed[d] = [
            send(
                pf.at[slot(near(d), lax.rem(b + e, nb))],
                rbuf.at[d, e - 1],
                rep,
                slot(a, lax.rem(b + e, nb)),
            )
            for e in range(1, nb)
        ]
    along = []
    for d in order:
        total = pf32[slot(near(d), b)]
        for e, copy in enumerate(crossed[d]):
            copy.wait_recv()
            total = total + rbuf[d, e].astype(F32)
        if d:
            sbuf[d - 1] = total.astype(BF16)
            along.append(send(sbuf.at[d - 1], fbuf.at[d - 1], rep, slot(near(d), b)))
    for d, copy in enumerate(along):
        copy.wait_recv()
        total = total + fbuf[d].astype(F32)
    fin[...] = total.astype(BF16)
    last = send(fin, land, to_rep, to_seg, start=False)

    @pl.when(jnp.logical_not(alone))
    def _():
        last.start()
        last.wait()
        out_ref[...] = land[...]

    @pl.when(alone)
    def _():
        out_ref[...] = fin[...]

    for copy in started:
        copy.wait_send()


def per_device(
    decoder_rows,
    norm_gain,
    query_weight,
    key_codes,
    key_scale,
    value_codes,
    value_scale,
    enc_lengths,
    output_weight,
):
    nseg, nrep = lax.axis_size("seg"), lax.axis_size("rep")
    nrow, c = decoder_rows.shape
    heads = key_scale.shape[2]
    tokens, inner = key_codes.shape[1:]
    assert key_codes.shape[0] == 1 and nseg % nrep == 0 and nseg % INNER_RING == 0
    na, nb = nseg // INNER_RING, INNER_RING
    copies = 2 + 2 * (nseg - 1) + 2 * (nrep - 1) + (nseg - 1) + na * (nb - 1) + na - 1
    vmem, smem, hbm = (
        pl.BlockSpec(memory_space=pltpu.VMEM),
        pl.BlockSpec(memory_space=pltpu.SMEM),
        pl.BlockSpec(memory_space=pl.ANY),
    )
    return pl.pallas_call(
        functools.partial(kernel, nseg, nrep, heads),
        out_shape=jax.ShapeDtypeStruct((nrow, c), BF16),
        in_specs=[vmem, vmem, hbm, hbm, smem, hbm, smem, smem, hbm],
        out_specs=vmem,
        scratch_shapes=[
            pltpu.VMEM(query_weight.shape, BF16),
            pltpu.VMEM(output_weight.shape, BF16),
            pltpu.VMEM((tokens, inner), BF16),
            pltpu.VMEM((tokens, inner), BF16),
            pltpu.VMEM((nseg, nrow, c), BF16),
            pltpu.VMEM((nrep * nrow, query_weight.shape[0]), BF16),
            pltpu.VMEM((nrep, nrow, c + LANES), BF16),
            pltpu.VMEM((nrep - 1, nrow, c + LANES), BF16),
            pltpu.VMEM((nseg, nrow, c), BF16),
            pltpu.VMEM((nseg, nrow, c + LANES), BF16),
            pltpu.VMEM((nseg - 1, nrow, c + LANES), BF16),
            pltpu.VMEM((nrep, nrow, c), BF16),
            pltpu.VMEM((nseg, nrow, c), BF16),
            pltpu.VMEM((nseg, nrow, c), F32),
            pltpu.VMEM((na, nb - 1, nrow, c), BF16),
            pltpu.VMEM((na - 1, nrow, c), BF16),
            pltpu.VMEM((na - 1, nrow, c), BF16),
            pltpu.VMEM((nrow, c), BF16),
            pltpu.VMEM((nrow, c), BF16),
            pltpu.SemaphoreType.DMA((4,)),
            pltpu.SemaphoreType.DMA((copies,)),
            pltpu.SemaphoreType.DMA((copies,)),
        ],
        compiler_params=pltpu.CompilerParams(
            collective_id=0, has_side_effects=True, vmem_limit_bytes=60 * 1024 * 1024
        ),
    )(
        decoder_rows,
        norm_gain.reshape(1, -1),
        query_weight,
        key_codes,
        key_scale,
        value_codes,
        value_scale,
        enc_lengths,
        output_weight,
    )


def solution(mesh):
    placed = (
        P("rep", "seg"),
        P(),
        P("rep", "seg"),
        P("rep", "seg", None),
        P("rep", "seg", None),
        P("rep", "seg", None),
        P("rep", "seg", None),
        P("rep"),
        P("seg", "rep"),
    )
    return jax.shard_map(
        per_device, mesh=mesh, in_specs=placed, out_specs=P("rep", "seg"), check_vma=False
    )
```

time: 252 us -> 74.9 us (0.30)
  the two profiles are of different devices: /device:TPU:5 before, /device:TPU:1 now
where the time goes in v1:
time: 74.9 us; the launch traced here: 74.7 us
  Pallas kernels  72.5 us (97%)
  local copies, waits for them, and re-layouts  1.47 us (2%)
    pallas_call x1, Pallas kernels, per_device(): pl.pallas_call(functools.partial(kernel, nseg, nrep, heads), out_shape=ja...  72.5 us

profile of v1, /device:TPU:1, one launch (start us, length us, event | category | flops | bytes accessed | tf_op | source)
XLA Modules:
  0.0 74.7 jit_solution(8646843482556545393)
XLA Ops:
  0.7 72.5 %shard_map.91 = bf16[64,512]{1,0:T(8,128)(2,1)} custom-call(bf16[64,512]{1,0:T(8,128)(2,1)} %rows_ref.1, f32[1,4096]{1,0:T(1,128)} %bitcast.1, bf16[1024,512]{1,0:T(8,128)(2,1)} %wq_hbm.1, bf16[1,512,4096]{2,1,0:T(8,128)(2,1)} %k_hbm.1, f32[1,4,64]{2,1,0:T(4,128)} %ks_ref.1, bf16[1,512,4096]{2,1,0:T(8,128)(2,1)} %v_hbm.1, f32[1,4,64]{2,1,0:T(4,128)} %vs_ref.1, ...), custom_call_target="tpu_custom_call" | custom-call | tf_op jit(solution)/shard_map/pallas_call | solution.py:392
  73.2 1.5 %copy.12 = bf16[64,512]{1,0:T(8,128)(2,1)} copy(bf16[64,512]{1,0:T(8,128)(2,1)} %shard_map.91) | data formatting | bytes 131072

commit v2 on v1

--- a/solution.py
+++ b/solution.py
@@ -52,9 +52,14 @@
     y,
     pq,
     pq_in,
+    pq32,
+    squares,
+    inverse,
     qs,
     oout,
-    oin,
+    crossed_in,
+    merged,
+    merged_in,
     ag,
     pf,
     pf32,
@@ -71,6 +76,8 @@
     rep = lax.axis_index("rep")
     nrow, c = rows_ref.shape
     width = gain_ref.shape[1]
+    lane = lax.broadcasted_iota(jnp.int32, (nrow, LANES), 1)
+    diagonal = lane == lax.broadcasted_iota(jnp.int32, (nrow, LANES), 0)
     m = nseg // nrep
     nb = INNER_RING
     na = nseg // nb
@@ -142,11 +149,23 @@
     @pl.when(jnp.logical_not(alone))
     def _():
         first.start()
-        first.wait()
 
     @pl.when(alone)
     def _():
         xg[seg] = rows_ref[...]
+
+    wide = rows_ref[...].astype(F32)
+    column = jnp.sum(wide * wide, axis=1, keepdims=True)
+    across_lanes = jnp.sum(jnp.where(diagonal, column, 0.0), axis=0, keepdims=True)
+    squares[seg] = jnp.broadcast_to(across_lanes, squares.shape[1:])
+    shares = [
+        send(squares.at[seg], squares.at[seg], rep, lax.rem(seg + d, nseg))
+        for d in range(1, nseg)
+    ]
+
+    @pl.when(jnp.logical_not(alone))
+    def _():
+        first.wait()
 
     def slot(ai, bi):
         return ai * nb + bi
@@ -171,63 +190,67 @@
             for e in range(1, nb)
         ]
 
-    def gather(buf, use):
+    def gather(buf, use, meanwhile=None):
         across, along = gather_start(buf)
-        use(seg)
+        if meanwhile is not None:
+            meanwhile()
+        use(seg, 0, 0)
         waiting = [(copy, slot(a, lax.rem(b + nb - e, nb))) for e, copy in enumerate(across, 1)]
         for d, copy in enumerate(along, 1):
             copy.wait_recv()
             passed = pass_on(buf, d)
-            for other, block in waiting:
+            for e, (other, block) in enumerate(waiting, 1):
                 other.wait_recv()
-                use(block)
-            use(slot(from_(d), b))
+                use(block, d - 1, e)
+            use(slot(from_(d), b), d, 0)
             waiting = [
                 (other, slot(from_(d), lax.rem(b + nb - e, nb))) for e, other in enumerate(passed, 1)
             ]
-        for other, block in waiting:
+        for e, (other, block) in enumerate(waiting, 1):
             other.wait_recv()
-            use(block)
-
-    gather(xg, lambda block: None)
-
-    lane = lax.broadcasted_iota(jnp.int32, (nrow, LANES), 1)
+            use(block, na - 1, e)
+
+    def norms():
+        for copy in shares:
+            copy.wait_recv()
+        total = functools.reduce(jnp.add, [squares[i] for i in range(nseg)])
+        inverse[rep] = lax.rsqrt(total / width + 1e-06)
+        for d in range(1, nrep):
+            told.append(send(inverse.at[rep], inverse.at[rep], lax.rem(rep + d, nrep), seg))
+
+    told = []
+    gather(xg, lambda block, d, e: None, norms)
+    for copy in told:
+        copy.wait_recv()
+
     for doc in range(nrep):
-        total = jnp.zeros((nrow, 1), F32)
+        factor = jnp.sum(jnp.where(diagonal, inverse[doc][0:1], 0.0), axis=1, keepdims=True)
         for j in range(m):
-            wide = xg[doc * m + j].astype(F32)
-            total = total + jnp.sum(wide * wide, axis=1, keepdims=True)
             at = pl.multiple_of((rep * m + j) * c, LANES)
             y[doc * nrow : (doc + 1) * nrow, j * c : (j + 1) * c] = (
-                wide * gain_ref[0:1, pl.ds(at, c)]
+                xg[doc * m + j].astype(F32) * factor * gain_ref[0:1, pl.ds(at, c)]
             ).astype(BF16)
-        pq[doc, :, c:] = spread(jnp.where(lane == 0, total, 0.0))
     loads["wq"].wait()
     part = jnp.dot(y[...], wq[...], preferred_element_type=F32)
     for doc in range(nrep):
-        pq[doc, :, :c] = part[doc * nrow : (doc + 1) * nrow].astype(BF16)
+        piece = part[doc * nrow : (doc + 1) * nrow]
+        pq32[doc] = piece
+        pq[doc] = piece.astype(BF16)
     sums = []
     for d in range(1, nrep):
         other = lax.rem(rep + d, nrep)
         sums.append(send(pq.at[other], pq_in.at[d - 1], other, seg))
-    acc = pq[rep, :, :c].astype(F32)
-    squares = gather_spread(pq[rep, :, c:])
+    acc = pq32[rep]
     for d, copy in enumerate(sums):
         copy.wait_recv()
-        acc = acc + pq_in[d, :, :c].astype(F32)
-        squares = squares + gather_spread(pq_in[d, :, c:])
-    inverse = lax.rsqrt(squares[:, 0:1] / width + 1e-06)
-    qs[seg] = (acc * inverse).astype(BF16)
+        acc = acc + pq_in[d].astype(F32)
+    qs[seg] = acc.astype(BF16)
 
     loads["k"].wait()
     loads["v"].wait()
     position = seg * tokens + lax.broadcasted_iota(jnp.int32, (1, tokens), 1)
     bias = jnp.where(position < len_ref[0], 0.0, -1e30).astype(F32)
-    turns = []
-
     def attend(block):
-        own_turn = not turns
-
         def one(t, stats):
             at = pl.multiple_of(t * LANES, LANES)
             wat = pl.multiple_of(block * c + t * LANES, LANES)
@@ -283,24 +306,17 @@
             0, pairs, one, jnp.zeros((nrow, LANES), F32), unroll=2 if pairs % 2 == 0 else 1
         )
         oout[block, :, c:] = spread(stats)
-        if own_turn:
-            turns.append(None)
-        else:
-            turns.append(send(oout.at[block], oin.at[len(turns) - 1], rep, block))
-
-    gather(qs, attend)
-
-    for copy in turns[1:]:
-        copy.wait_recv()
-    parts = [oout.at[seg]] + [oin.at[i] for i in range(nseg - 1)]
-    stats = [gather_spread(part_ref[:, c:]) for part_ref in parts]
-    largest = functools.reduce(jnp.maximum, stats)
-    factors = [jnp.exp(s - largest) for s in stats]
-    denominator = functools.reduce(
-        jnp.add, [f * pltpu.roll(s, LANES // 2, 1) for f, s in zip(factors, stats)]
-    )
-    factors = [f / denominator for f in factors]
-    for t in range(pairs):
+
+    def merge(parts):
+        stats = [gather_spread(part_ref[:, c:]) for part_ref in parts]
+        largest = functools.reduce(jnp.maximum, stats)
+        factors = [jnp.exp(s - largest) for s in stats]
+        totals = functools.reduce(
+            jnp.add, [f * pltpu.roll(s, LANES // 2, 1) for f, s in zip(factors, stats)]
+        )
+        return factors, largest, totals
+
+    def mix(factors, parts, t):
         cut = slice(t * LANES, (t + 1) * LANES)
         total = None
         for f, part_ref in zip(factors, parts):
@@ -309,7 +325,45 @@
                 g = jnp.where(lane >= i * hd, f[:, t * hpl + i : t * hpl + i + 1], g)
             term = g * part_ref[:, cut].astype(F32)
             total = term if total is None else total + term
-        ag[rep, :, cut] = total.astype(BF16)
+        return total
+
+    crossing, moving = {}, []
+
+    def settle(d):
+        for copy in crossing[d]:
+            copy.wait_recv()
+        block = slot(from_(d), b)
+        parts = [oout.at[block]] + [crossed_in.at[d, e] for e in range(nb - 1)]
+        factors, largest, totals = merge(parts)
+        for t in range(pairs):
+            merged[d, :, t * LANES : (t + 1) * LANES] = mix(factors, parts, t).astype(BF16)
+        kept = jnp.where(lane < hpb, largest, 0.0)
+        kept = kept + pltpu.roll(jnp.where(lane < hpb, totals, 0.0), LANES // 2, 1)
+        merged[d, :, c:] = spread(kept)
+        if d:
+            moving.append(send(merged.at[d], merged_in.at[d - 1], rep, block))
+
+    def turn(block, d, e):
+        attend(block)
+        if e:
+            to = slot(a, lax.rem(b + nb - e, nb))
+            crossing.setdefault(d, []).append(
+                send(oout.at[block], crossed_in.at[d, e - 1], rep, to)
+            )
+            if e == nb - 1 and d >= 2:
+                settle(d - 1)
+
+    gather(qs, turn)
+    for d in [na - 1] * (na > 1) + [0]:
+        settle(d)
+
+    for copy in moving:
+        copy.wait_recv()
+    parts = [merged.at[0]] + [merged_in.at[i] for i in range(na - 1)]
+    factors, _, totals = merge(parts)
+    factors = [f / totals for f in factors]
+    for t in range(pairs):
+        ag[rep, :, t * LANES : (t + 1) * LANES] = mix(factors, parts, t).astype(BF16)
     shared = [
         send(ag.at[rep], ag.at[rep], lax.rem(rep + d, nrep), seg) for d in range(1, nrep)
     ]
@@ -383,7 +437,7 @@
     tokens, inner = key_codes.shape[1:]
     assert key_codes.shape[0] == 1 and nseg % nrep == 0 and nseg % INNER_RING == 0
     na, nb = nseg // INNER_RING, INNER_RING
-    copies = 2 + 2 * (nseg - 1) + 2 * (nrep - 1) + (nseg - 1) + na * (nb - 1) + na - 1
+    copies = 2 + 5 * (nseg - 1) + 3 * (nrep - 1)
     vmem, smem, hbm = (
         pl.BlockSpec(memory_space=pltpu.VMEM),
         pl.BlockSpec(memory_space=pltpu.SMEM),
@@ -401,11 +455,16 @@
             pltpu.VMEM((tokens, inner), BF16),
             pltpu.VMEM((nseg, nrow, c), BF16),
             pltpu.VMEM((nrep * nrow, query_weight.shape[0]), BF16),
-            pltpu.VMEM((nrep, nrow, c + LANES), BF16),
-            pltpu.VMEM((nrep - 1, nrow, c + LANES), BF16),
+            pltpu.VMEM((nrep, nrow, c), BF16),
+            pltpu.VMEM((nrep - 1, nrow, c), BF16),
+            pltpu.VMEM((nrep, nrow, c), F32),
+            pltpu.VMEM((nseg, 8, LANES), F32),
+            pltpu.VMEM((nrep, 8, LANES), F32),
             pltpu.VMEM((nseg, nrow, c), BF16),
             pltpu.VMEM((nseg, nrow, c + LANES), BF16),
-            pltpu.VMEM((nseg - 1, nrow, c + LANES), BF16),
+            pltpu.VMEM((na, nb - 1, nrow, c + LANES), BF16),
+            pltpu.VMEM((na, nrow, c + LANES), BF16),
+            pltpu.VMEM((na - 1, nrow, c + LANES), BF16),
             pltpu.VMEM((nrep, nrow, c), BF16),
             pltpu.VMEM((nseg, nrow, c), BF16),
             pltpu.VMEM((nseg, nrow, c), F32),

time: 74.9 us -> 73.8 us (0.985)
  the two profiles are of different devices: /device:TPU:1 before, /device:TPU:5 now
where the time goes in v2:
time: 73.8 us; the launch traced here: 73.6 us
  Pallas kernels  71.5 us (97%)
  local copies, waits for them, and re-layouts  1.47 us (2%)
    pallas_call x1, Pallas kernels, per_device(): pl.pallas_call(functools.partial(kernel, nseg, nrep, heads), out_shape=ja...  71.5 us

profile of v2, /device:TPU:5, one launch (start us, length us, event | category | flops | bytes accessed | tf_op | source)
XLA Modules:
  0.0 73.6 jit_solution(13394721049140158017)
XLA Ops:
  0.7 71.5 %shard_map.91 = bf16[64,512]{1,0:T(8,128)(2,1)} custom-call(bf16[64,512]{1,0:T(8,128)(2,1)} %rows_ref.1, f32[1,4096]{1,0:T(1,128)} %bitcast.1, bf16[1024,512]{1,0:T(8,128)(2,1)} %wq_hbm.1, bf16[1,512,4096]{2,1,0:T(8,128)(2,1)} %k_hbm.1, f32[1,4,64]{2,1,0:T(4,128)} %ks_ref.1, bf16[1,512,4096]{2,1,0:T(8,128)(2,1)} %v_hbm.1, f32[1,4,64]{2,1,0:T(4,128)} %vs_ref.1, ...), custom_call_target="tpu_custom_call" | custom-call | tf_op jit(solution)/shard_map/pallas_call | solution.py:446
  72.1 1.5 %copy.12 = bf16[64,512]{1,0:T(8,128)(2,1)} copy(bf16[64,512]{1,0:T(8,128)(2,1)} %shard_map.91) | data formatting | bytes 131072

commit v3 on v2

v3 whole, which is shorter than its diff:
```python
import functools

import jax
import jax.numpy as jnp
from jax import lax
from jax.experimental import pallas as pl
from jax.experimental.pallas import tpu as pltpu
from jax.sharding import PartitionSpec as P

F32 = jnp.float32
BF16 = jnp.bfloat16
LANES = 128
PART = 16
INNER_RING = 2
HALVES = 2


def spread(value):
    high = value.astype(BF16).astype(F32)
    rest = value - high
    mid = rest.astype(BF16).astype(F32)
    low = (rest - mid).astype(BF16).astype(F32)
    packed = high + pltpu.roll(mid, PART, 1) + pltpu.roll(low, 2 * PART, 1)
    return packed.astype(BF16)


def gather_spread(packed):
    wide = packed.astype(F32)
    low = pltpu.roll(wide, LANES - 2 * PART, 1)
    mid = pltpu.roll(wide, LANES - PART, 1)
    return wide + (mid + low)


def kernel(
    nseg,
    nrep,
    heads,
    rows_ref,
    gain_ref,
    wq_hbm,
    k_hbm,
    ks_ref,
    v_hbm,
    vs_ref,
    len_ref,
    wo_hbm,
    out_ref,
    wq,
    wo,
    kbuf,
    vbuf,
    xg,
    y,
    pq,
    pq_in,
    pq32,
    squares,
    inverse,
    qs,
    oout,
    crossed_in,
    merged,
    merged_in,
    ag,
    pf,
    pf32,
    rbuf,
    sbuf,
    fbuf,
    fin,
    land,
    local_sem,
    send_sem,
    recv_sem,
):
    seg = lax.axis_index("seg")
    rep = lax.axis_index("rep")
    all_rows, c = rows_ref.shape
    nrow = all_rows // HALVES
    width = gain_ref.shape[1]
    lane = lax.broadcasted_iota(jnp.int32, (nrow, LANES), 1)

    def diagonal(count, first_row):
        shape = (count, LANES)
        return lax.broadcasted_iota(jnp.int32, shape, 1) == first_row + lax.broadcasted_iota(
            jnp.int32, shape, 0
        )

    m = nseg // nrep
    nb = INNER_RING
    na = nseg // nb
    a, b = seg // nb, seg % nb
    hd = wq.shape[1] * nseg // heads
    hpl = LANES // hd
    hpb = c // hd
    pairs = c // LANES
    tokens = kbuf.shape[0]
    blocks = ks_ref.shape[1]
    blen = tokens // blocks

    state = {"k": 0}
    started = []

    def send(src, dst, to_rep, to_seg, start=True):
        k = state["k"]
        state["k"] += 1
        copy = pltpu.make_async_remote_copy(
            src_ref=src,
            dst_ref=dst,
            send_sem=send_sem.at[k],
            recv_sem=recv_sem.at[k],
            device_id={"rep": to_rep, "seg": to_seg},
            device_id_type=pl.DeviceIdType.MESH,
        )
        if start:
            copy.start()
            started.append(copy)
        return copy

    loads = {}
    lk = 0

    def load(name, src, dst):
        nonlocal lk
        copy = pltpu.make_async_copy(src, dst, local_sem.at[lk])
        lk += 1
        copy.start()
        loads[name] = copy

    load("wq", wq_hbm, wq)
    load("k", k_hbm.at[0], kbuf)
    load("v", v_hbm.at[0], vbuf)
    load("wo", wo_hbm, wo)

    to_rep, to_seg = seg // m, rep * m + seg % m
    alone = to_rep == rep
    barrier = pltpu.get_barrier_semaphore()

    def greet(r, s):
        pl.semaphore_signal(
            barrier, inc=1, device_id={"rep": r, "seg": s}, device_id_type=pl.DeviceIdType.MESH
        )

    for d in range(1, nseg):
        greet(rep, lax.rem(seg + d, nseg))
    for d in range(1, nrep):
        greet(lax.rem(rep + d, nrep), seg)

    @pl.when(jnp.logical_not(alone))
    def _():
        greet(to_rep, to_seg)

    pl.semaphore_wait(barrier, jnp.where(alone, nseg + nrep - 2, nseg + nrep - 1))

    firsts = [
        send(rows_ref.at[pl.ds(h * nrow, nrow)], xg.at[h, to_seg], to_rep, to_seg, start=False)
        for h in range(HALVES)
    ]

    @pl.when(jnp.logical_not(alone))
    def _():
        for first in firsts:
            first.start()

    @pl.when(alone)
    def _():
        for h in range(HALVES):
            xg[h, seg] = rows_ref[h * nrow : (h + 1) * nrow]

    wide = rows_ref[...].astype(F32)
    column = jnp.sum(wide * wide, axis=1, keepdims=True)
    across_lanes = jnp.sum(jnp.where(diagonal(all_rows, 0), column, 0.0), axis=0, keepdims=True)
    squares[seg] = jnp.broadcast_to(across_lanes, squares.shape[1:])
    shares = [
        send(squares.at[seg], squares.at[seg], rep, lax.rem(seg + d, nseg))
        for d in range(1, nseg)
    ]

    def slot(ai, bi):
        return ai * nb + bi

    def near(d):
        return lax.rem(a + d, na)

    def from_(d):
        return lax.rem(a + na - d, na)

    def gather_start(buf):
        across = [
            send(buf.at[seg], buf.at[seg], rep, slot(a, lax.rem(b + e, nb))) for e in range(1, nb)
        ]
        along = [send(buf.at[seg], buf.at[seg], rep, slot(near(d), b)) for d in range(1, na)]
        return across, along

    def pass_on(buf, d):
        block = slot(from_(d), b)
        return [
            send(buf.at[block], buf.at[block], rep, slot(a, lax.rem(b + e, nb)))
            for e in range(1, nb)
        ]

    def gather(buf, use, meanwhile=None):
        across, along = gather_start(buf)
        yield
        if meanwhile is not None:
            meanwhile()
        use(seg, 0, 0)
        waiting = [(copy, slot(a, lax.rem(b + nb - e, nb))) for e, copy in enumerate(across, 1)]
        for d, copy in enumerate(along, 1):
            copy.wait_recv()
            passed = pass_on(buf, d)
            for e, (other, block) in enumerate(waiting, 1):
                other.wait_recv()
                use(block, d - 1, e)
            yield
            use(slot(from_(d), b), d, 0)
            yield
            waiting = [
                (other, slot(from_(d), lax.rem(b + nb - e, nb))) for e, other in enumerate(passed, 1)
            ]
        for e, (other, block) in enumerate(waiting, 1):
            other.wait_recv()
            use(block, na - 1, e)

    def norms():
        for copy in shares:
            copy.wait_recv()
        total = functools.reduce(jnp.add, [squares[i] for i in range(nseg)])
        inverse[rep] = lax.rsqrt(total / width + 1e-06)
        for d in range(1, nrep):
            told.append(send(inverse.at[rep], inverse.at[rep], lax.rem(rep + d, nrep), seg))

    told = []
    known = []

    position = seg * tokens + lax.broadcasted_iota(jnp.int32, (1, tokens), 1)
    bias = jnp.where(position < len_ref[0], 0.0, -1e30).astype(F32)

    def once(name):
        if name in loads:
            loads.pop(name).wait()

    def chain(h, xg, y, pq, pq_in, pq32, qs, oout, crossed_in, merged, merged_in, ag, pf, pf32, rbuf, sbuf, fbuf, fin, land):
        @pl.when(jnp.logical_not(alone))
        def _():
            firsts[h].wait()

        yield from gather(xg, lambda block, d, e: None, norms if h == 0 else None)
        if not known:
            known.append(None)
            for copy in told:
                copy.wait_recv()

        for doc in range(nrep):
            factor = jnp.sum(jnp.where(diagonal(nrow, h * nrow), inverse[doc][0:1], 0.0), axis=1, keepdims=True)
            for j in range(m):
                at = pl.multiple_of((rep * m + j) * c, LANES)
                y[doc * nrow : (doc + 1) * nrow, j * c : (j + 1) * c] = (
                    xg[doc * m + j].astype(F32) * factor * gain_ref[0:1, pl.ds(at, c)]
                ).astype(BF16)
        once("wq")
        part = jnp.dot(y[...], wq[...], preferred_element_type=F32)
        for doc in range(nrep):
            piece = part[doc * nrow : (doc + 1) * nrow]
            pq32[doc] = piece
            pq[doc] = piece.astype(BF16)
        sums = []
        for d in range(1, nrep):
            other = lax.rem(rep + d, nrep)
            sums.append(send(pq.at[other], pq_in.at[d - 1], other, seg))
        yield
        acc = pq32[rep]
        for d, copy in enumerate(sums):
            copy.wait_recv()
            acc = acc + pq_in[d].astype(F32)
        qs[seg] = acc.astype(BF16)

        once("k")
        once("v")
        def attend(block):
            def one(t, stats):
                at = pl.multiple_of(t * LANES, LANES)
                wat = pl.multiple_of(block * c + t * LANES, LANES)
                q = qs[block, :, pl.ds(at, LANES)]
                stacked = jnp.concatenate(
                    [
                        jnp.where((lane >= i * hd) & (lane < (i + 1) * hd), q, jnp.zeros_like(q))
                        for i in range(hpl)
                    ],
                    axis=0,
                )
                scores = lax.dot_general(
                    stacked,
                    kbuf[:, pl.ds(wat, LANES)],
                    (((1,), (1,)), ((), ())),
                    preferred_element_type=F32,
                )
                scaled_rows = []
                for i in range(hpl):
                    head = block * hpb + t * hpl + i
                    pieces = []
                    for n in range(blocks):
                        cut = slice(n * blen, (n + 1) * blen)
                        pieces.append(
                            scores[i * nrow : (i + 1) * nrow, cut] * ks_ref[0, n, head]
                            + bias[:, cut]
                        )
                    top = functools.reduce(jnp.maximum, pieces)
                    peak = jnp.max(top, axis=1, keepdims=True)
                    weights = [jnp.exp(piece - peak) for piece in pieces]
                    whole = jnp.sum(functools.reduce(jnp.add, weights), axis=1, keepdims=True)
                    scaled_rows.append(
                        jnp.concatenate(
                            [(w * vs_ref[0, n, head]).astype(BF16) for n, w in enumerate(weights)],
                            axis=1,
                        )
                    )
                    index = t * hpl + i
                    stats = jnp.where(lane == index, peak, stats)
                    stats = jnp.where(lane == LANES // 2 + index, whole, stats)
                summed = jnp.dot(
                    jnp.concatenate(scaled_rows, axis=0),
                    vbuf[:, pl.ds(wat, LANES)],
                    preferred_element_type=F32,
                )
                mine = summed[:nrow]
                for i in range(1, hpl):
                    mine = jnp.where(lane >= i * hd, summed[i * nrow : (i + 1) * nrow], mine)
                oout[block, :, pl.ds(at, LANES)] = mine.astype(BF16)
                return stats

            stats = lax.fori_loop(
                0, pairs, one, jnp.zeros((nrow, LANES), F32), unroll=2 if pairs % 2 == 0 else 1
            )
            oout[block, :, c:] = spread(stats)

        def merge(parts):
            stats = [gather_spread(part_ref[:, c:]) for part_ref in parts]
            largest = functools.reduce(jnp.maximum, stats)
            factors = [jnp.exp(s - largest) for s in stats]
            totals = functools.reduce(
                jnp.add, [f * pltpu.roll(s, LANES // 2, 1) for f, s in zip(factors, stats)]
            )
            return factors, largest, totals

        def mix(factors, parts, t):
            cut = slice(t * LANES, (t + 1) * LANES)
            total = None
            for f, part_ref in zip(factors, parts):
                g = f[:, t * hpl : t * hpl + 1]
                for i in range(1, hpl):
                    g = jnp.where(lane >= i * hd, f[:, t * hpl + i : t * hpl + i + 1], g)
                term = g * part_ref[:, cut].astype(F32)
                total = term if total is None else total + term
            return total

        crossing, moving = {}, []

        def settle(d):
            for copy in crossing[d]:
                copy.wait_recv()
            block = slot(from_(d), b)
            parts = [oout.at[block]] + [crossed_in.at[d, e] for e in range(nb - 1)]
            factors, largest, totals = merge(parts)
            for t in range(pairs):
                merged[d, :, t * LANES : (t + 1) * LANES] = mix(factors, parts, t).astype(BF16)
            kept = jnp.where(lane < hpb, largest, 0.0)
            kept = kept + pltpu.roll(jnp.where(lane < hpb, totals, 0.0), LANES // 2, 1)
            merged[d, :, c:] = spread(kept)
            if d:
                moving.append(send(merged.at[d], merged_in.at[d - 1], rep, block))

        def turn(block, d, e):
            attend(block)
            if e:
                to = slot(a, lax.rem(b + nb - e, nb))
                crossing.setdefault(d, []).append(
                    send(oout.at[block], crossed_in.at[d, e - 1], rep, to)
                )
                if e == nb - 1 and d >= 2:
                    settle(d - 1)

        yield from gather(qs, turn)
        for d in [na - 1] * (na > 1) + [0]:
            yield
            settle(d)
        yield

        for copy in moving:
            copy.wait_recv()
        parts = [merged.at[0]] + [merged_in.at[i] for i in range(na - 1)]
        factors, _, totals = merge(parts)
        factors = [f / totals for f in factors]
        for t in range(pairs):
            ag[rep, :, t * LANES : (t + 1) * LANES] = mix(factors, parts, t).astype(BF16)
        shared = [
            send(ag.at[rep], ag.at[rep], lax.rem(rep + d, nrep), seg) for d in range(1, nrep)
        ]
        once("wo")
        yield
        for copy in shared:
            copy.wait_recv()

        part = jnp.dot(
            ag[...].reshape(nrep * nrow, c), wo[...], preferred_element_type=F32
        )
        for p in range(nseg):
            doc, j = p // m, p % m
            piece = part[doc * nrow : (doc + 1) * nrow, j * c : (j + 1) * c]
            pf32[p] = piece
            pf[p] = piece.astype(BF16)
        order = list(range(1, na)) + [0]
        crossed = {}
        for d in order:
            crossed[d] = [
                send(
                    pf.at[slot(near(d), lax.rem(b + e, nb))],
                    rbuf.at[d, e - 1],
                    rep,
                    slot(a, lax.rem(b + e, nb)),
                )
                for e in range(1, nb)
            ]
        along = []
        for d in order:
            yield
            total = pf32[slot(near(d), b)]
            for e, copy in enumerate(crossed[d]):
                copy.wait_recv()
                total = total + rbuf[d, e].astype(F32)
            if d:
                sbuf[d - 1] = total.astype(BF16)
                along.append(send(sbuf.at[d - 1], fbuf.at[d - 1], rep, slot(near(d), b)))
        yield
        for d, copy in enumerate(along):
            copy.wait_recv()
            total = total + fbuf[d].astype(F32)
        fin[...] = total.astype(BF16)
        last = send(fin, land, to_rep, to_seg, start=False)
        mine = pl.ds(h * nrow, nrow)

        @pl.when(jnp.logical_not(alone))
        def _():
            last.start()

        yield

        @pl.when(jnp.logical_not(alone))
        def _():
            last.wait()
            out_ref[mine, :] = land[...]

        @pl.when(alone)
        def _():
            out_ref[mine, :] = fin[...]


    state_refs = [xg, y, pq, pq_in, pq32, qs, oout, crossed_in, merged, merged_in, ag, pf, pf32, rbuf, sbuf, fbuf, fin, land]
    chains = [chain(h, *[ref.at[h] for ref in state_refs]) for h in range(HALVES)]
    while chains:
        for steps in list(chains):
            try:
                next(steps)
            except StopIteration:
                chains.remove(steps)
    for name in list(loads):
        once(name)
    for copy in started:
        copy.wait_send()


def per_device(
    decoder_rows,
    norm_gain,
    query_weight,
    key_codes,
    key_scale,
    value_codes,
    value_scale,
    enc_lengths,
    output_weight,
):
    nseg, nrep = lax.axis_size("seg"), lax.axis_size("rep")
    nrow, c = decoder_rows.shape
    heads = key_scale.shape[2]
    tokens, inner = key_codes.shape[1:]
    assert key_codes.shape[0] == 1 and nseg % nrep == 0 and nseg % INNER_RING == 0
    na, nb = nseg // INNER_RING, INNER_RING
    copies = HALVES * (2 + 4 * (nseg - 1) + 2 * (nrep - 1)) + nseg - 1 + nrep - 1
    part = nrow // HALVES

    def half(shape, dtype=BF16):
        return pltpu.VMEM((HALVES,) + shape, dtype)

    vmem, smem, hbm = (
        pl.BlockSpec(memory_space=pltpu.VMEM),
        pl.BlockSpec(memory_space=pltpu.SMEM),
        pl.BlockSpec(memory_space=pl.ANY),
    )
    return pl.pallas_call(
        functools.partial(kernel, nseg, nrep, heads),
        out_shape=jax.ShapeDtypeStruct((nrow, c), BF16),
        in_specs=[vmem, vmem, hbm, hbm, smem, hbm, smem, smem, hbm],
        out_specs=vmem,
        scratch_shapes=[
            pltpu.VMEM(query_weight.shape, BF16),
            pltpu.VMEM(output_weight.shape, BF16),
            pltpu.VMEM((tokens, inner), BF16),
            pltpu.VMEM((tokens, inner), BF16),
            half((nseg, part, c)),
            half((nrep * part, query_weight.shape[0])),
            half((nrep, part, c)),
            half((nrep - 1, part, c)),
            half((nrep, part, c), F32),
            pltpu.VMEM((nseg, 8, LANES), F32),
            pltpu.VMEM((nrep, 8, LANES), F32),
            half((nseg, part, c)),
            half((nseg, part, c + LANES)),
            half((na, nb - 1, part, c + LANES)),
            half((na, part, c + LANES)),
            half((na - 1, part, c + LANES)),
            half((nrep, part, c)),
            half((nseg, part, c)),
            half((nseg, part, c), F32),
            half((na, nb - 1, part, c)),
            half((na - 1, part, c)),
            half((na - 1, part, c)),
            half((part, c)),
            half((part, c)),
            pltpu.SemaphoreType.DMA((4,)),
            pltpu.SemaphoreType.DMA((copies,)),
            pltpu.SemaphoreType.DMA((copies,)),
        ],
        compiler_params=pltpu.CompilerParams(
            collective_id=0, has_side_effects=True, vmem_limit_bytes=60 * 1024 * 1024
        ),
    )(
        decoder_rows,
        norm_gain.reshape(1, -1),
        query_weight,
        key_codes,
        key_scale,
        value_codes,
        value_scale,
        enc_lengths,
        output_weight,
    )


def solution(mesh):
    placed = (
        P("rep", "seg"),
        P(),
        P("rep", "seg"),
        P("rep", "seg", None),
        P("rep", "seg", None),
        P("rep", "seg", None),
        P("rep", "seg", None),
        P("rep"),
        P("seg", "rep"),
    )
    return jax.shard_map(
        per_device, mesh=mesh, in_specs=placed, out_specs=P("rep", "seg"), check_vma=False
    )
```

time: 73.8 us -> 79.1 us (1.072)
  Pallas kernels: 71.5 us -> 76.8 us
    pallas_call x1, Pallas kernels: 71.5 us -> 76.8 us  [per_device(): pl.pallas_call(functools.partial(kernel, nseg, nrep, heads), out_shape=ja...]
where the time goes in v3:
time: 79.1 us; the launch traced here: 78.9 us
  Pallas kernels  76.8 us (97%)
  local copies, waits for them, and re-layouts  1.47 us (2%)
    pallas_call x1, Pallas kernels, per_device(): pl.pallas_call(functools.partial(kernel, nseg, nrep, heads), out_shape=ja...  76.8 us

profile of v3, /device:TPU:5, one launch (start us, length us, event | category | flops | bytes accessed | tf_op | source)
XLA Modules:
  0.0 78.9 jit_solution(16557239644600368445)
XLA Ops:
  0.7 76.8 %shard_map.91 = bf16[64,512]{1,0:T(8,128)(2,1)} custom-call(bf16[64,512]{1,0:T(8,128)(2,1)} %rows_ref.1, f32[1,4096]{1,0:T(1,128)} %bitcast.1, bf16[1024,512]{1,0:T(8,128)(2,1)} %wq_hbm.1, bf16[1,512,4096]{2,1,0:T(8,128)(2,1)} %k_hbm.1, f32[1,4,64]{2,1,0:T(4,128)} %ks_ref.1, bf16[1,512,4096]{2,1,0:T(8,128)(2,1)} %v_hbm.1, f32[1,4,64]{2,1,0:T(4,128)} %vs_ref.1, ...), custom_call_target="tpu_custom_call" | custom-call | tf_op jit(solution)/shard_map/pallas_call | solution.py:500
  77.5 1.5 %copy.12 = bf16[64,512]{1,0:T(8,128)(2,1)} copy(bf16[64,512]{1,0:T(8,128)(2,1)} %shard_map.91) | data formatting | bytes 131072

commit v4 on v2

--- a/solution.py
+++ b/solution.py
@@ -171,10 +171,17 @@
         return ai * nb + bi
 
     def near(d):
-        return lax.rem(a + d, na)
+        if na & (na - 1):
+            return lax.rem(a + d, na)
+        flipped, bit = 0, 1
+        while bit < na:
+            own = (a // bit) % 2
+            flipped = flipped + bit * ((1 - own) if d & bit else own)
+            bit *= 2
+        return flipped
 
     def from_(d):
-        return lax.rem(a + na - d, na)
+        return lax.rem(a + na - d, na) if na & (na - 1) else near(d)
 
     def gather_start(buf):
         across = [
@@ -379,7 +386,7 @@
         piece = part[doc * nrow : (doc + 1) * nrow, j * c : (j + 1) * c]
         pf32[p] = piece
         pf[p] = piece.astype(BF16)
-    order = list(range(1, na)) + [0]
+    order = list(range(na - 1, -1, -1))
     crossed = {}
     for d in order:
         crossed[d] = [
@@ -400,8 +407,9 @@
         if d:
             sbuf[d - 1] = total.astype(BF16)
             along.append(send(sbuf.at[d - 1], fbuf.at[d - 1], rep, slot(near(d), b)))
-    for d, copy in enumerate(along):
+    for copy in along:
         copy.wait_recv()
+    for d in range(na - 1):
         total = total + fbuf[d].astype(F32)
     fin[...] = total.astype(BF16)
     last = send(fin, land, to_rep, to_seg, start=False)

time: 73.8 us -> 73.6 us (level)
  no operation moved by 1% of the time
where the time goes in v4:
time: 73.6 us; the launch traced here: 73.4 us
  Pallas kernels  71.3 us (97%)
  local copies, waits for them, and re-layouts  1.47 us (2%)
    pallas_call x1, Pallas kernels, per_device(): pl.pallas_call(functools.partial(kernel, nseg, nrep, heads), out_shape=ja...  71.3 us
    unnamed x1, local copies, waits for them, and re-layouts  1.47 us

profile of v4, /device:TPU:5, one launch (start us, length us, event | category | flops | bytes accessed | tf_op | source)
XLA Modules:
  0.0 73.4 jit_solution(15060611835611134850)
XLA Ops:
  0.7 71.3 %shard_map.91 = bf16[64,512]{1,0:T(8,128)(2,1)} custom-call(bf16[64,512]{1,0:T(8,128)(2,1)} %rows_ref.1, f32[1,4096]{1,0:T(1,128)} %bitcast.1, bf16[1024,512]{1,0:T(8,128)(2,1)} %wq_hbm.1, bf16[1,512,4096]{2,1,0:T(8,128)(2,1)} %k_hbm.1, f32[1,4,64]{2,1,0:T(4,128)} %ks_ref.1, bf16[1,512,4096]{2,1,0:T(8,128)(2,1)} %v_hbm.1, f32[1,4,64]{2,1,0:T(4,128)} %vs_ref.1, ...), custom_call_target="tpu_custom_call" | custom-call | tf_op jit(solution)/shard_map/pallas_call | solution.py:454
  71.9 1.5 %copy.12 = bf16[64,512]{1,0:T(8,128)(2,1)} copy(bf16[64,512]{1,0:T(8,128)(2,1)} %shard_map.91) | data formatting | bytes 131072
